TPU v7x, 32 devices: a whole 2x2x4 slice. The times are simulated.
32 devices in a mesh: fsdp: 8 (over z, x), rep: 4 (over y, core).
Axes of the slice: x: 2, y: 2, z: 4, core: 2. Of those that a mesh axis runs over, the one named last changes fastest.
Arguments:
- samples: bfloat16 [768, 4096], P(('fsdp', 'rep')), may hold values from -10 to 10
- dual_weight: bfloat16 [8192, 4096], P('fsdp'), may hold values from -0.09375 to 0.09375
- dual_vector: float32 [2, 8192], P(None, 'fsdp'), may hold values from 0 to 2
- map_weight: float32 [8192, 4096], P(('fsdp', 'rep')), may hold values from -0.09375 to 0.09375
- map_vector: float32 [2, 8192], P(None, ('fsdp', 'rep')), may hold values from 0.001 to 2
- moment_weight: float32 [8192, 4096], P(('fsdp', 'rep')), may hold values from -0.006 to 0.006
- square_weight: float32 [8192, 4096], P(('fsdp', 'rep')), may hold values from 0.0001 to 0.01
- moment_vector: float32 [2, 8192], P(None, ('fsdp', 'rep')), may hold values from -0.03 to 0.03
- square_vector: float32 [2, 8192], P(None, ('fsdp', 'rep')), may hold values from 0.0001 to 0.01
Outputs:
- next_weight: float32 [8192, 4096], P(('fsdp', 'rep'))
- next_vector: float32 [2, 8192], P(None, ('fsdp', 'rep'))
- next_moment_weight: float32 [8192, 4096], P(('fsdp', 'rep'))
- next_square_weight: float32 [8192, 4096], P(('fsdp', 'rep'))
- next_moment_vector: float32 [2, 8192], P(None, ('fsdp', 'rep'))
- next_square_vector: float32 [2, 8192], P(None, ('fsdp', 'rep'))
All inputs are finite; a program needn't handle non-finite values.
Results may differ from a plain program's by a relative error of at most 0.004.
Values may be sent and summed in bfloat16 or wider, within the bound.
A program may use at most 128 MiB of HBM per device.

v0:
```python
import jax
import jax.numpy as jnp
from jax import lax
from jax.sharding import PartitionSpec as P

beta_one = 0.9
beta_two = 0.999
learn_rate = 0.001
epsilon = 1e-08
adam_step = 10


def contract_last(left, right):
    return lax.dot_general(
        left, right, (((1,), (1,)), ((), ())), preferred_element_type=jnp.float32
    )


def contract_first(left, right):
    return lax.dot_general(
        left, right, (((0,), (0,)), ((), ())), preferred_element_type=jnp.float32
    )


def adam_update(param, grad, moment, square):
    moment_new = beta_one * moment + (1.0 - beta_one) * grad
    square_new = beta_two * square + (1.0 - beta_two) * grad * grad
    fix_one = 1.0 - beta_one**adam_step
    fix_two = 1.0 - beta_two**adam_step
    update = learn_rate * (moment_new / fix_one) / (jnp.sqrt(square_new / fix_two) + epsilon)
    return (param - update, moment_new, square_new)


def body(
    samples,
    dual_weight,
    dual_vector,
    map_weight,
    map_vector,
    moment_weight,
    square_weight,
    moment_vector,
    square_vector,
):
    group_rows = lax.all_gather(samples, "fsdp", axis=0, tiled=True)
    weight_slab, vector_slab = (
        lax.all_gather(map_weight.astype(jnp.bfloat16), "rep", axis=0, tiled=True),
        lax.all_gather(map_vector.astype(jnp.bfloat16), "rep", axis=1, tiled=True),
    )
    readout = vector_slab[0].astype(jnp.float32)
    offset = vector_slab[1].astype(jnp.float32)
    inverse_rows = 1.0 / (group_rows.shape[0] * lax.axis_size("rep"))
    hidden = contract_last(group_rows, weight_slab) + offset
    sigma = jax.nn.sigmoid(hidden)
    scaled = (readout * sigma).astype(jnp.bfloat16)
    group_float = group_rows.astype(jnp.float32)
    mapped = group_float + lax.psum(
        jnp.dot(scaled, weight_slab, preferred_element_type=jnp.float32).astype(jnp.bfloat16),
        "fsdp",
    ).astype(jnp.float32)
    mapped_low = mapped.astype(jnp.bfloat16)
    dual_hidden = contract_last(mapped_low, dual_weight) + dual_vector[1]
    dual_scaled = (dual_vector[0] * jax.nn.sigmoid(dual_hidden)).astype(jnp.bfloat16)
    dual_grad = mapped + lax.psum(
        jnp.dot(dual_scaled, dual_weight, preferred_element_type=jnp.float32).astype(jnp.bfloat16),
        "fsdp",
    ).astype(jnp.float32)
    residual = (group_float - dual_grad).astype(jnp.bfloat16)
    pulled = contract_last(residual, weight_slab)
    slope = sigma * (1.0 - sigma)
    curve_float = readout * slope * pulled
    curve_term = curve_float.astype(jnp.bfloat16)
    left_stack = jnp.concatenate([scaled, curve_term], axis=0)
    right_stack = jnp.concatenate([residual, group_rows], axis=0)
    grad_slab = contract_first(left_stack, right_stack) * inverse_rows
    grad_small = (
        jnp.stack([jnp.sum(sigma * pulled, axis=0), jnp.sum(curve_float, axis=0)]) * inverse_rows
    )
    owner_weight, owner_vector = (
        lax.psum_scatter(grad_slab, "rep", scatter_dimension=0, tiled=True),
        lax.psum_scatter(grad_small, "rep", scatter_dimension=1, tiled=True),
    )
    next_weight, next_moment_weight, next_square_weight = adam_update(
        map_weight, owner_weight, moment_weight, square_weight
    )
    raw_vector, next_moment_vector, next_square_vector = adam_update(
        map_vector, owner_vector, moment_vector, square_vector
    )
    next_vector = jnp.concatenate([jnp.maximum(raw_vector[0:1], 0.0), raw_vector[1:2]], axis=0)
    return (
        next_weight,
        next_vector,
        next_moment_weight,
        next_square_weight,
        next_moment_vector,
        next_square_vector,
    )


def solution(mesh):
    return jax.shard_map(
        body,
        mesh=mesh,
        in_specs=(
            P(("fsdp", "rep"), None),
            P("fsdp", None),
            P(None, "fsdp"),
            P(("fsdp", "rep"), None),
            P(None, ("fsdp", "rep")),
            P(("fsdp", "rep"), None),
            P(("fsdp", "rep"), None),
            P(None, ("fsdp", "rep")),
            P(None, ("fsdp", "rep")),
        ),
        out_specs=(
            P(("fsdp", "rep"), None),
            P(None, ("fsdp", "rep")),
            P(("fsdp", "rep"), None),
            P(("fsdp", "rep"), None),
            P(None, ("fsdp", "rep")),
            P(None, ("fsdp", "rep")),
        ),
        check_vma=False,
    )
```

profile of v0, /device:TPU:0, one launch (start us, length us, event | category | flops | bytes accessed | tf_op | source)
XLA Modules:
  0.0 494.8 jit_solution(3073785880574631769)
XLA Ops:
  7.2 0.7 all-gather.3.cloned.1.call-update
  8.0 3.8 convert_element_type.41
  11.8 0.0 all-reduce.3.cloned.1.call-start
  11.8 6.0 %all_gather.9 = bf16[2,1024]{1,0:T(2,128)(2,1)S(1)} all-gather(bf16[2,256]{1,0:T(2,128)(2,1)S(1)} %convert_element_type.40), channel_id=1, replica_groups=mesh['fsdp'=8,'rep'=4] {'rep'}, dimensions={1}, use_global_device_ids=true | all-gather | bytes 5120 | tf_op jit(solution)/shard_map/all_gather | solution.py:48
  17.9 39.2 %all-gather.3.cloned.1.call-done = bf16[192,4096]{1,0:T(8,128)(2,1)} async-done(((bf16[24,4096]{1,0:T(8,128)(2,1)}), bf16[192,4096]{1,0:T(8,128)(2,1)}) %all-gather.3.cloned.1.call-update) | async-done | bytes 1572880 | tf_op jit(solution)/shard_map/all_gather | solution.py:45
  57.1 58.8 %all-gather.5.cloned.1.call-done = bf16[1024,4096]{1,0:T(8,128)(2,1)} async-done(((bf16[256,4096]{1,0:T(8,128)(2,1)}), bf16[1024,4096]{1,0:T(8,128)(2,1)}) %all-gather.5.cloned.1.call-update) | async-done | bytes 8388624 | tf_op jit(solution)/shard_map/all_gather | solution.py:47
  115.9 7.9 %multiply_convert_fusion = (bf16[192,1024]{1,0:T(8,128)(2,1)S(1)}, f32[192,1024]{1,0:T(8,128)}) fusion(f32[1024]{0:T(1024)S(1)} %bitcast.18, f32[1024]{0:T(1024)S(1)} %bitcast.20, bf16[192,4096]{1,0:T(8,128)(2,1)} %all-gather.3.cloned.1.call-done, bf16[1024,4096]{1,0:T(8,128)(2,1)} %all-gather.5.cloned.1.call-done), kind=kOutput, calls=%fused_computation.34 | convolution fusion | flops 1611792384 | bytes 11149312 | tf_op jit(solution)/shard_map/dot_general | solution.py:14
  123.8 3.0 convolution_convert_fusion.1
  126.8 0.0 all-reduce.5.cloned.1.call-start
  126.9 89.3 %all-reduce.3.cloned.1.call-done = bf16[192,4096]{1,0:T(8,128)(2,1)} async-done(((bf16[192,4096]{1,0:T(8,128)(2,1)}), bf16[192,4096]{1,0:T(8,128)(2,1)}) %all-reduce.3.cloned.1.call-update) | async-done | bytes 1572880 | tf_op jit(solution)/shard_map/psum | solution.py:57
  216.2 12.0 %convolution_convert_fusion = bf16[192,4096]{1,0:T(8,128)(2,1)} fusion(bf16[1024,4096]{1,0:T(8,128)(2,1)} %param.10, bf16[192,4096]{1,0:T(8,128)(2,1)} %all-reduce.3.cloned.1.call-done, bf16[192,4096]{1,0:T(8,128)(2,1)S(1)} %copy-done, f32[1024]{0:T(1024)S(1)} %bitcast.22, f32[1024]{0:T(1024)S(1)} %bitcast.21), kind=kOutput, calls=%fused_computation.2 | convolution fusion | flops 3226337280 | bytes 13115392 | tf_op jit(solution)/shard_map/dot_general | solution.py:65
  228.2 0.0 reduce-scatter.7.cloned.1.call-start
  228.3 88.6 %all-reduce.5.cloned.1.call-done = bf16[192,4096]{1,0:T(8,128)(2,1)} async-done(((bf16[192,4096]{1,0:T(8,128)(2,1)}), bf16[192,4096]{1,0:T(8,128)(2,1)}) %all-reduce.5.cloned.1.call-update) | async-done | bytes 1572880 | tf_op jit(solution)/shard_map/psum | solution.py:64
  316.9 2.7 fusion.1
  319.6 7.2 %multiply_reduce_fusion = (f32[1024]{0:T(1024)S(1)}, f32[1024]{0:T(1024)S(1)}, bf16[192,1024]{1,0:T(8,128)(2,1)}) fusion(f32[192,1024]{1,0:T(8,128)} %get-tuple-element.22, f32[1024]{0:T(1024)S(1)} %bitcast.19, bf16[192,4096]{1,0:T(8,128)(2,1)S(1)} %fusion.1, bf16[1024,4096]{1,0:T(8,128)(2,1)} %all-gather.5.cloned.1.call-done), kind=kOutput, calls=%fused_computation.33 | convolution fusion | flops 1612183552 | bytes 11153408 | tf_op jit(solution)/shard_map/dot_general | solution.py:14
  326.9 1.0 copy.15
  327.9 0.2 reduce-scatter.5.cloned.1.call-start
  328.1 9.2 %convolution_multiply_fusion = f32[1024,4096]{1,0:T(8,128)} fusion(bf16[192,4096]{1,0:T(8,128)(2,1)S(1)} %copy-done, bf16[192,4096]{1,0:T(8,128)(2,1)S(1)} %fusion.1, bf16[192,1024]{1,0:T(8,128)(2,1)} %get-tuple-element.14, bf16[192,1024]{1,0:T(8,128)(2,1)S(1)} %get-tuple-element.21), kind=kOutput, calls=%fused_computation | convolution fusion | flops 3233284096 | bytes 20709376 | tf_op jit(solution)/shard_map/dot_general | solution.py:20
  337.4 11.6 %reduce-scatter.7.cloned.1.call-done = f32[256,2]{1,0:T(8,128)} async-done(((f32[1024,2]{1,0:T(8,128)}), f32[256,2]{1,0:T(8,128)}) %reduce-scatter.7.cloned.1.call-update) | async-done | bytes 2064
  349.0 1.0 copy.16
  350.0 0.6 divide_subtract_fusion.1
  350.6 0.6 pad_maximum_fusion
  351.2 125.3 %reduce-scatter.5.cloned.1.call-done = f32[256,4096]{1,0:T(8,128)} async-done(((f32[1024,4096]{1,0:T(8,128)}), f32[256,4096]{1,0:T(8,128)}) %reduce-scatter.5.cloned.1.call-update) | async-done | bytes 4194320 | tf_op jit(solution)/shard_map/reduce_scatter | solution.py:80
  476.5 11.4 %divide_subtract_fusion = (f32[256,4096]{1,0:T(8,128)}, f32[256,4096]{1,0:T(8,128)}, f32[256,4096]{1,0:T(8,128)}) fusion(f32[256,4096]{1,0:T(8,128)} %param.12, f32[256,4096]{1,0:T(8,128)} %reduce-scatter.5.cloned.1.call-done, f32[256,4096]{1,0:T(8,128)} %param.14, f32[256,4096]{1,0:T(8,128)} %param.15), kind=kLoop, calls=%fused_computation.5 | loop fusion | flops 12582912 | bytes 29360128 | tf_op jit(solution)/shard_map/sub | solution.py:31
  (24 shorter events, 0.2 us)
Async XLA Ops:
  7.2 49.9 %all-gather.3.cloned.1.call-start = ((), (), s32[]{:S(2)}) async-start(), calls=%async_computation.2 | async-start | bytes 1769472 | tf_op jit(solution)/shard_map/all_gather | solution.py:45
  7.9 3.9 copy-start.1
  7.9 108.0 %all-gather.5.cloned.1.call-start = ((), (), s32[]{:S(2)}) async-start(), calls=%async_computation.3 | async-start | bytes 10485760 | tf_op jit(solution)/shard_map/all_gather | solution.py:47
  11.8 204.5 %all-reduce.3.cloned.1.call-start = ((), (), s32[]{:S(2)}) async-start(), calls=%async_computation.4 | async-start | bytes 3145728 | tf_op jit(solution)/shard_map/psum | solution.py:57
  115.9 7.9 %copy-start.5 = (bf16[1024,4096]{1,0:T(8,128)(2,1)S(1)}, bf16[1024,4096]{1,0:T(8,128)(2,1)}, u32[]{:S(2)}) copy-start(bf16[1024,4096]{1,0:T(8,128)(2,1)} %all-gather.5.cloned.1.call-done) | copy-start | bytes 25165828
  123.8 3.1 copy-start.2
  123.8 92.5 %copy-start = (bf16[192,4096]{1,0:T(8,128)(2,1)S(1)}, bf16[192,4096]{1,0:T(8,128)(2,1)}, u32[]{:S(2)}) copy-start(bf16[192,4096]{1,0:T(8,128)(2,1)} %all-gather.3.cloned.1.call-done) | copy-start | bytes 4718596
  126.8 190.1 %all-reduce.5.cloned.1.call-start = ((), (), s32[]{:S(2)}) async-start(), calls=%async_computation.5 | async-start | bytes 3145728 | tf_op jit(solution)/shard_map/psum | solution.py:64
  228.2 120.8 %reduce-scatter.7.cloned.1.call-start = ((), (), s32[]{:S(2)}) async-start(), calls=%async_computation.7 | async-start | bytes 655360
  327.9 148.6 %reduce-scatter.5.cloned.1.call-start = ((), (), s32[]{:S(2)}) async-start(), calls=%async_computation.6 | async-start | bytes 20971520 | tf_op jit(solution)/shard_map/reduce_scatter | solution.py:80
  337.4 12.6 %copy-start.3 = (f32[2,256]{1,0:T(2,128)S(1)}, f32[2,256]{1,0:T(2,128)}, u32[]{:S(2)}) copy-start(f32[2,256]{1,0:T(2,128)} %param.16) | copy-start | bytes 6148
  337.4 12.6 %copy-start.4 = (f32[2,256]{1,0:T(2,128)S(1)}, f32[2,256]{1,0:T(2,128)}, u32[]{:S(2)}) copy-start(f32[2,256]{1,0:T(2,128)} %param.17) | copy-start | bytes 6148
Sparse Core Ops, SparseCore 0:
  10.2 46.8 all-gather.2
  59.2 56.6 all-gather.4
  126.9 89.2 all-reduce.2
  228.4 88.5 all-reduce.4
  328.0 20.9 reduce-scatter.6
  351.4 125.0 reduce-scatter.4
where the time goes:
time: 495 us
  waiting for transfers between devices  414 us (84%)
  matrix products  39.3 us (8%)
  other arithmetic  19.1 us (4%)
  between operations  14.2 us (3%)
  blocking collectives  6.04 us (1%)
    reduce_scatter x1, waiting for transfers between devices, body(): lax.psum_scatter(grad_slab, 'rep', scatter_dimension=0, tiled=True)  125 us
    psum x1, waiting for transfers between devices, body(): lax.psum(jnp.dot(scaled, weight_slab, preferred_element_type=jnp.float32)...  89.3 us
    psum x1, waiting for transfers between devices, body(): lax.psum(jnp.dot(dual_scaled, dual_weight, preferred_element_type=jnp.flo...  88.6 us
    all_gather x1, waiting for transfers between devices, body(): lax.all_gather(map_weight.astype(jnp.bfloat16), 'rep', axis=0, tiled=True)  58.8 us
    all_gather x1, waiting for transfers between devices, body(): group_rows = lax.all_gather(samples, 'fsdp', axis=0, tiled=True)  39.2 us
    dot_general x2, matrix products, contract_last(): lax.dot_general(left, right, (((1,), (1,)), ((), ())), preferred_element_...  15.1 us
    unnamed x7, waiting for transfers between devices  12.4 us
    sub x2, other arithmetic, adam_update(): return (param - update, moment_new, square_new)  12 us
  transfers between devices with their start and end apart: 6, of which 6 were waited for; matrix products, arithmetic and copies ran while one was open for 3% of the time, Pallas kernels for 0%

commit v1 on v0

--- a/solution.py
+++ b/solution.py
@@ -54,9 +54,12 @@
     sigma = jax.nn.sigmoid(hidden)
     scaled = (readout * sigma).astype(jnp.bfloat16)
     group_float = group_rows.astype(jnp.float32)
-    mapped = group_float + lax.psum(
-        jnp.dot(scaled, weight_slab, preferred_element_type=jnp.float32).astype(jnp.bfloat16),
-        "fsdp",
+    mapped = group_float + jnp.sum(
+        lax.all_gather(
+            jnp.dot(scaled, weight_slab, preferred_element_type=jnp.float32).astype(jnp.bfloat16),
+            "fsdp",
+        ),
+        axis=0,
     ).astype(jnp.float32)
     mapped_low = mapped.astype(jnp.bfloat16)
     dual_hidden = contract_last(mapped_low, dual_weight) + dual_vector[1]

time: 495 us -> 588 us (1.19)
  waiting for transfers between devices: 414 us -> 499 us
  other arithmetic: 19.1 us -> 26.4 us
    all_gather x0 -> x1, waiting for transfers between devices: none -> 176 us  [body(): lax.all_gather(jnp.dot(scaled, weight_slab, preferred_element_type=jnp.fl...]
    psum x1 -> x0, waiting for transfers between devices: 89.3 us -> none  [body(): lax.psum(jnp.dot(scaled, weight_slab, preferred_element_type=jnp.float32)...]
    reduce_sum x0 -> x1, other arithmetic: none -> 7.15 us  [body(): jnp.sum(lax.all_gather(jnp.dot(scaled, weight_slab, preferred_element_typ...]
where the time goes in v1:
time: 588 us
  waiting for transfers between devices  499 us (85%)
  matrix products  39.4 us (7%)
  other arithmetic  26.4 us (4%)
  between operations  14.2 us (2%)
  blocking collectives  6.04 us (1%)
    all_gather x1, waiting for transfers between devices, body(): lax.all_gather(jnp.dot(scaled, weight_slab, preferred_element_type=jnp.fl...  176 us
    reduce_scatter x1, waiting for transfers between devices, body(): lax.psum_scatter(grad_slab, 'rep', scatter_dimension=0, tiled=True)  125 us
    psum x1, waiting for transfers between devices, body(): lax.psum(jnp.dot(dual_scaled, dual_weight, preferred_element_type=jnp.flo...  87.4 us
    all_gather x1, waiting for transfers between devices, body(): lax.all_gather(map_weight.astype(jnp.bfloat16), 'rep', axis=0, tiled=True)  58.8 us
    all_gather x1, waiting for transfers between devices, body(): group_rows = lax.all_gather(samples, 'fsdp', axis=0, tiled=True)  39.2 us
    dot_general x2, matrix products, contract_last(): lax.dot_general(left, right, (((1,), (1,)), ((), ())), preferred_element_...  15 us
    unnamed x7, waiting for transfers between devices  12.5 us
    dot_general x1, matrix products, body(): jnp.dot(dual_scaled, dual_weight, preferred_element_type=jnp.float32)  12.1 us
  transfers between devices with their start and end apart: 6, of which 6 were waited for; matrix products, arithmetic and copies ran while one was open for 3% of the time, Pallas kernels for 0%

profile of v1, /device:TPU:0, one launch (start us, length us, event | category | flops | bytes accessed | tf_op | source)
XLA Modules:
  0.0 587.8 jit_solution(11808772259298278218)
XLA Ops:
  7.2 0.7 all-gather.5.cloned.1.call-update
  8.0 3.8 convert_element_type.43
  11.8 0.0 all-gather.9.cloned.1.call-start
  11.8 6.0 %all_gather.15 = bf16[2,1024]{1,0:T(2,128)(2,1)S(1)} all-gather(bf16[2,256]{1,0:T(2,128)(2,1)S(1)} %convert_element_type.42), channel_id=1, replica_groups=mesh['fsdp'=8,'rep'=4] {'rep'}, dimensions={1}, use_global_device_ids=true | all-gather | bytes 5120 | tf_op jit(solution)/shard_map/all_gather | solution.py:48
  17.9 39.2 %all-gather.5.cloned.1.call-done = bf16[192,4096]{1,0:T(8,128)(2,1)} async-done(((bf16[24,4096]{1,0:T(8,128)(2,1)}), bf16[192,4096]{1,0:T(8,128)(2,1)}) %all-gather.5.cloned.1.call-update) | async-done | bytes 1572880 | tf_op jit(solution)/shard_map/all_gather | solution.py:45
  57.1 58.8 %all-gather.7.cloned.1.call-done = bf16[1024,4096]{1,0:T(8,128)(2,1)} async-done(((bf16[256,4096]{1,0:T(8,128)(2,1)}), bf16[1024,4096]{1,0:T(8,128)(2,1)}) %all-gather.7.cloned.1.call-update) | async-done | bytes 8388624 | tf_op jit(solution)/shard_map/all_gather | solution.py:47
  115.9 7.9 %multiply_convert_fusion = (bf16[192,1024]{1,0:T(8,128)(2,1)S(1)}, f32[192,1024]{1,0:T(8,128)}) fusion(f32[1024]{0:T(1024)S(1)} %bitcast.20, f32[1024]{0:T(1024)S(1)} %bitcast.22, bf16[192,4096]{1,0:T(8,128)(2,1)} %all-gather.5.cloned.1.call-done, bf16[1024,4096]{1,0:T(8,128)(2,1)} %all-gather.7.cloned.1.call-done), kind=kOutput, calls=%fused_computation.34 | convolution fusion | flops 1611792384 | bytes 11149312 | tf_op jit(solution)/shard_map/dot_general | solution.py:14
  123.8 3.0 convolution_convert_fusion.1
  126.9 0.6 fusion.50
  127.5 175.6 %all-gather.9.cloned.1.call-done = bf16[1536,4096]{1,0:T(8,128)(2,1)} async-done(((bf16[192,4096]{1,0:T(8,128)(2,1)}), bf16[1536,4096]{1,0:T(8,128)(2,1)}) %all-gather.9.cloned.1.call-update) | async-done | bytes 12582928 | tf_op jit(solution)/shard_map/all_gather | solution.py:58
  303.1 7.2 %reduce_sum.30 = bf16[192,4096]{1,0:T(8,128)(2,1)S(1)} reduce(bf16[8,192,4096]{2,1,0:T(8,128)(2,1)} %bitcast.17, bf16[]{:T(256)} %constant.13.clone.1), dimensions={0}, to_apply=%region_0.0 | reduce | flops 5505024 | bytes 14155778 | tf_op jit(solution)/shard_map/reduce_sum | solution.py:57
  310.3 12.1 %convolution_convert_fusion = bf16[192,4096]{1,0:T(8,128)(2,1)} fusion(bf16[1024,4096]{1,0:T(8,128)(2,1)} %param.10, bf16[192,4096]{1,0:T(8,128)(2,1)S(1)} %reduce_sum.30, bf16[192,4096]{1,0:T(8,128)(2,1)S(1)} %copy-done, f32[1024]{0:T(1024)S(1)} %bitcast.24, f32[1024]{0:T(1024)S(1)} %bitcast.23), kind=kOutput, calls=%fused_computation.2 | convolution fusion | flops 3226337280 | bytes 13115392 | tf_op jit(solution)/shard_map/dot_general | solution.py:68
  322.4 0.2 reduce-scatter.7.cloned.1.call-start
  322.6 87.4 %all-reduce.2.cloned.1.call-done = bf16[192,4096]{1,0:T(8,128)(2,1)} async-done(((bf16[192,4096]{1,0:T(8,128)(2,1)}), bf16[192,4096]{1,0:T(8,128)(2,1)}) %all-reduce.2.cloned.1.call-update) | async-done | bytes 1572880 | tf_op jit(solution)/shard_map/psum | solution.py:67
  410.0 2.8 fusion.1
  412.8 7.1 %multiply_reduce_fusion = (f32[1024]{0:T(1024)S(1)}, f32[1024]{0:T(1024)S(1)}, bf16[192,1024]{1,0:T(8,128)(2,1)}) fusion(f32[192,1024]{1,0:T(8,128)S(1)} %copy-done.9, f32[1024]{0:T(1024)S(1)} %bitcast.21, bf16[192,4096]{1,0:T(8,128)(2,1)S(1)} %fusion.1, bf16[1024,4096]{1,0:T(8,128)(2,1)} %all-gather.7.cloned.1.call-done), kind=kOutput, calls=%fused_computation.33 | convolution fusion | flops 1612183552 | bytes 11153408 | tf_op jit(solution)/shard_map/dot_general | solution.py:14
  419.9 1.0 copy.15
  421.0 9.3 %convolution_multiply_fusion = f32[1024,4096]{1,0:T(8,128)} fusion(bf16[192,4096]{1,0:T(8,128)(2,1)S(1)} %copy-done, bf16[192,4096]{1,0:T(8,128)(2,1)S(1)} %fusion.1, bf16[192,1024]{1,0:T(8,128)(2,1)} %get-tuple-element.14, bf16[192,1024]{1,0:T(8,128)(2,1)S(1)} %get-tuple-element.21), kind=kOutput, calls=%fused_computation | convolution fusion | flops 3233284096 | bytes 20709376 | tf_op jit(solution)/shard_map/dot_general | solution.py:20
  430.3 11.7 %reduce-scatter.7.cloned.1.call-done = f32[256,2]{1,0:T(8,128)} async-done(((f32[1024,2]{1,0:T(8,128)}), f32[256,2]{1,0:T(8,128)}) %reduce-scatter.7.cloned.1.call-update) | async-done | bytes 2064
  442.0 1.0 copy.16
  443.0 0.6 divide_subtract_fusion.1
  443.6 0.6 pad_maximum_fusion
  444.2 125.3 %reduce-scatter.5.cloned.1.call-done = f32[256,4096]{1,0:T(8,128)} async-done(((f32[1024,4096]{1,0:T(8,128)}), f32[256,4096]{1,0:T(8,128)}) %reduce-scatter.5.cloned.1.call-update) | async-done | bytes 4194320 | tf_op jit(solution)/shard_map/reduce_scatter | solution.py:83
  569.5 11.4 %divide_subtract_fusion = (f32[256,4096]{1,0:T(8,128)}, f32[256,4096]{1,0:T(8,128)}, f32[256,4096]{1,0:T(8,128)}) fusion(f32[256,4096]{1,0:T(8,128)} %param.12, f32[256,4096]{1,0:T(8,128)} %reduce-scatter.5.cloned.1.call-done, f32[256,4096]{1,0:T(8,128)} %param.14, f32[256,4096]{1,0:T(8,128)} %param.15), kind=kLoop, calls=%fused_computation.5 | loop fusion | flops 12582912 | bytes 29360128 | tf_op jit(solution)/shard_map/sub | solution.py:31
  (33 shorter events, 0.3 us)
Async XLA Ops:
  7.2 49.9 %all-gather.5.cloned.1.call-start = ((), (), s32[]{:S(2)}) async-start(), calls=%async_computation.2 | async-start | bytes 1769472 | tf_op jit(solution)/shard_map/all_gather | solution.py:45
  7.9 3.9 copy-start.2
  7.9 108.0 %all-gather.7.cloned.1.call-start = ((), (), s32[]{:S(2)}) async-start(), calls=%async_computation.3 | async-start | bytes 10485760 | tf_op jit(solution)/shard_map/all_gather | solution.py:47
  11.8 291.3 %all-gather.9.cloned.1.call-start = ((), (), s32[]{:S(2)}) async-start(), calls=%async_computation.6 | async-start | bytes 14155776 | tf_op jit(solution)/shard_map/all_gather | solution.py:58
  115.9 7.9 %copy-start.8 = (bf16[1024,4096]{1,0:T(8,128)(2,1)S(1)}, bf16[1024,4096]{1,0:T(8,128)(2,1)}, u32[]{:S(2)}) copy-start(bf16[1024,4096]{1,0:T(8,128)(2,1)} %all-gather.7.cloned.1.call-done) | copy-start | bytes 25165828
  123.8 3.1 copy-start.3
  126.8 283.2 %all-reduce.2.cloned.1.call-start = ((), (), s32[]{:S(2)}) async-start(), calls=%async_computation.4 | async-start | bytes 3145728 | tf_op jit(solution)/shard_map/psum | solution.py:67
  303.1 7.2 %copy-start = (bf16[192,4096]{1,0:T(8,128)(2,1)S(1)}, bf16[192,4096]{1,0:T(8,128)(2,1)}, u32[]{:S(2)}) copy-start(bf16[192,4096]{1,0:T(8,128)(2,1)} %all-gather.5.cloned.1.call-done) | copy-start | bytes 4718596
  303.1 7.2 %copy-start.4 = (f32[1,1024]{1,0:T(1,128)S(1)}, f32[1,1024]{1,0:T(1,128)}, u32[]{:S(2)}) copy-start(f32[1,1024]{1,0:T(1,128)} %get-tuple-element.15) | copy-start | bytes 12292
  303.1 7.2 %copy-start.5 = (f32[1,1024]{1,0:T(1,128)S(1)}, f32[1,1024]{1,0:T(1,128)}, u32[]{:S(2)}) copy-start(f32[1,1024]{1,0:T(1,128)} %get-tuple-element.16) | copy-start | bytes 12292
  310.2 12.1 %copy-start.1 = (bf16[192,4096]{1,0:T(8,128)(2,1)}, bf16[192,4096]{1,0:T(8,128)(2,1)S(1)}, u32[]{:S(2)}) copy-start(bf16[192,4096]{1,0:T(8,128)(2,1)S(1)} %reduce_sum.30) | copy-start | bytes 4718596
  322.4 119.7 %reduce-scatter.7.cloned.1.call-start = ((), (), s32[]{:S(2)}) async-start(), calls=%async_computation.7 | async-start | bytes 655360
  410.0 2.8 copy-start.9
  420.9 148.6 %reduce-scatter.5.cloned.1.call-start = ((), (), s32[]{:S(2)}) async-start(), calls=%async_computation.5 | async-start | bytes 20971520 | tf_op jit(solution)/shard_map/reduce_scatter | solution.py:83
  430.3 12.7 %copy-start.6 = (f32[2,256]{1,0:T(2,128)S(1)}, f32[2,256]{1,0:T(2,128)}, u32[]{:S(2)}) copy-start(f32[2,256]{1,0:T(2,128)} %param.16) | copy-start | bytes 6148
  430.3 12.7 %copy-start.7 = (f32[2,256]{1,0:T(2,128)S(1)}, f32[2,256]{1,0:T(2,128)}, u32[]{:S(2)}) copy-start(f32[2,256]{1,0:T(2,128)} %param.17) | copy-start | bytes 6148
Sparse Core Ops, SparseCore 0:
  10.2 46.8 all-gather.4
  59.2 56.6 all-gather.6
  126.9 176.0 all-gather.8
  322.5 87.4 all-reduce.1
  421.1 20.9 reduce-scatter.6
  444.5 125.0 reduce-scatter.4
